TPU v7x, 32 devices: a whole 2x2x4 slice. The times are simulated.
32 devices in a mesh: blk: 16 (over z, y, core), rep: 2 (over x).
Axes of the slice: x: 2, y: 2, z: 4, core: 2. Of those that a mesh axis runs over, the one named last changes fastest.
Arguments:
- grad_out: bfloat16 [24576, 256], P('blk'), may hold values from -6 to 6
- pre_act: bfloat16 [24576, 256], P('blk'), may hold values from -6 to 6
- prev_pre: bfloat16 [24576, 256], P(('blk', 'rep')), may hold values from -6 to 6
- weight: bfloat16 [256, 256], replicated, may hold values from -0.375 to 0.375
- block_values: bfloat16 [3840, 128, 128], P(('blk', 'rep')), may hold values from -0.25 to 0.25
- block_rows: int32 [3840], P(('blk', 'rep')), may hold values from 0 to 11, as said below
- block_cols: int32 [3840], P(('blk', 'rep')), may hold values from 0 to 59
Outputs:
- grad_in: bfloat16 [24576, 256], P(('blk', 'rep'))
- grad_weight: float32 [256, 256], replicated
Inputs may be any that keep to these rules, and one draw needn't show every extreme that they name: The blocks of the 2 devices of one stripe sit at distinct (block_rows, block_cols) positions.
All inputs are finite; a program needn't handle non-finite values.
Results may differ from a plain program's by a relative error of at most 0.0049.
Values sent between devices are 32-bit elements; how exact they have to be, the bound alone decides.
A program may use at most 192 MiB of HBM per device.

v0:
```python
import math
import jax
import jax.numpy as jnp
from jax import lax
from jax.sharding import PartitionSpec as P

HALO = 2


def shifted(value, axis, by):
    devices = lax.axis_size(axis)
    return lax.ppermute(value, axis, [(i, (i + by) % devices) for i in range(devices)])


def local(grad_out, pre_act, prev_pre, weight, block_values, block_rows, block_cols):
    stripe_rows, width = grad_out.shape
    block_size = block_values.shape[1]
    stripe_blocks = stripe_rows // block_size
    spans = 2 * HALO + 1
    masked = grad_out * (pre_act > 0).astype(jnp.bfloat16)
    picked = masked.reshape(stripe_blocks, block_size, width)[block_rows]
    tiles = jnp.einsum("kab,kaf->kbf", block_values, picked, preferred_element_type=jnp.float32)
    window = jax.ops.segment_sum(tiles, block_cols, num_segments=spans * stripe_blocks)
    window = window.reshape(spans, stripe_rows, width)
    total = window[HALO]
    for position in range(spans):
        if position != HALO:
            total = total + shifted(window[position], "blk", position - HALO)
    mine = lax.psum_scatter(total, "rep", scatter_dimension=0, tiled=True)
    dy_rows = mine.astype(jnp.bfloat16)
    feats = jnp.maximum(prev_pre, jnp.zeros_like(prev_pre))
    weight_term = jnp.dot(feats.T, dy_rows, preferred_element_type=jnp.float32)
    node_count = stripe_rows * lax.axis_size("blk")
    grad_weight = lax.psum(weight_term, ("blk", "rep")) * (1.0 / math.sqrt(node_count))
    grad_in = (
        jnp.dot(dy_rows, weight.T, preferred_element_type=jnp.float32)
        * (prev_pre > 0).astype(jnp.float32)
    ).astype(jnp.bfloat16)
    return (grad_in, grad_weight)


def solution(mesh):
    in_specs = (
        P("blk", None),
        P("blk", None),
        P(("blk", "rep"), None),
        P(),
        P(("blk", "rep"), None, None),
        P(("blk", "rep")),
        P(("blk", "rep")),
    )
    out_specs = (P(("blk", "rep"), None), P())
    return jax.shard_map(local, mesh=mesh, in_specs=in_specs, out_specs=out_specs, check_vma=False)
```

profile of v0, /device:TPU:0, one launch (start us, length us, event | category | flops | bytes accessed | tf_op | source)
XLA Modules:
  0.0 365.0 jit_solution(13241581030041668142)
XLA Ops:
  7.2 0.0 copy-start
  7.2 0.0 reduce-scatter.2.cloned.1.call-start
  7.2 0.7 compare_select_fusion.1
  7.9 1.5 compare_select_fusion
  9.4 6.4 %gather_fusion = bf16[120,128,256]{2,1,0:T(8,128)(2,1)} fusion(bf16[12,128,256]{2,1,0:T(8,128)(2,1)S(1)} %bitcast.18, s32[1024]{0:T(1024)S(1)} %pad_clamp_fusion), kind=kCustom, calls=%fused_computation | custom fusion | bytes 15729120 | tf_op jit(solution)/shard_map/gather | solution.py:21
  15.8 12.1 %convolution_bitcast_fusion = f32[120,128,256]{1,2,0:T(8,128)} fusion(bf16[120,128,256]{2,1,0:T(8,128)(2,1)} %gather_fusion, bf16[120,128,128]{2,1,0:T(8,128)(2,1)} %param.11), kind=kOutput, calls=%fused_computation.2 | convolution fusion | flops 1006632960 | bytes 27525120 | tf_op jit(solution)/shard_map/kab,kaf->kbf/dot_general | solution.py:22
  27.9 15.6 %copy.11 = f32[120,128,256]{2,1,0:T(8,128)} copy(f32[120,128,256]{1,2,0:T(8,128)} %convolution_bitcast_fusion) | data formatting | bytes 31457280 | tf_op jit(solution)/shard_map/kab,kaf->kbf/dot_general | solution.py:22
  43.5 0.0 copy-start.3
  43.5 4.1 %broadcast_in_dim.9 = f32[60,128,256]{2,1,0:T(8,128)} broadcast(f32[]{:T(128)} %constant.2.clone.1), dimensions={} | broadcast | bytes 7864324 | tf_op jit(solution)/shard_map/broadcast_in_dim | solution.py:23
  47.5 0.0 copy-done.3
  47.5 38.0 %scatter_fusion = f32[60,128,256]{2,1,0:T(8,128)} fusion(f32[60,128,256]{2,1,0:T(8,128)} %broadcast_in_dim.9, s32[120]{0:T(128)S(1)} %copy-done.3, f32[120,128,256]{2,1,0:T(8,128)} %copy.11), kind=kCustom, calls=%fused_computation.1 | custom fusion | flops 3932160 | bytes 47186400 | tf_op jit(solution)/shard_map/scatter-add | solution.py:23
  85.6 3.9 %fusion.10 = (f32[12,128,256]{2,1,0:T(8,128)S(1)}, f32[12,128,256]{2,1,0:T(8,128)S(1)}, f32[12,128,256]{2,1,0:T(8,128)S(1)}, f32[12,128,256]{2,1,0:T(8,128)S(1)}, f32[12,128,256]{2,1,0:T(8,128)S(1)}) fusion(f32[60,128,256]{2,1,0:T(8,128)} %scatter_fusion), kind=kLoop, calls=%fused_computation.19 | loop fusion | bytes 15728640 | tf_op jit(solution)/shard_map/slice | solution.py:25
  89.4 3.0 collective-permute-start.3
  92.5 0.0 collective-permute-start.2
  92.5 4.4 %collective-permute-start.1 = (f32[1536,256]{1,0:T(8,128)S(1)}, f32[1536,256]{1,0:T(8,128)S(1)}, u32[]{:S(2)}, u32[]{:S(2)}) collective-permute-start(f32[1536,256]{1,0:T(8,128)S(1)} %bitcast.20), channel_id=1, source_target_pairs={{0,30},{2,0},{4,2},{6,4},{8,6},{10,8},{12,10},{14,12},{16,14},{18,... | collective-permute-start | bytes 4718600 | tf_op jit(solution)/shard_map/ppermute | solution.py:12
  96.9 0.3 collective-permute-start
  97.2 80.6 %collective-permute-done.3 = f32[1536,256]{1,0:T(8,128)S(1)} collective-permute-done((f32[1536,256]{1,0:T(8,128)S(1)}, f32[1536,256]{1,0:T(8,128)S(1)}, u32[]{:S(2)}, u32[]{:S(2)}) %collective-permute-start.3) | collective-permute-done | bytes 1572896 | tf_op jit(solution)/shard_map/ppermute | solution.py:12
  177.8 0.0 collective-permute-done.2
  177.8 0.0 collective-permute-done.1
  177.8 19.3 %collective-permute-done = f32[1536,256]{1,0:T(8,128)S(1)} collective-permute-done((f32[1536,256]{1,0:T(8,128)S(1)}, f32[1536,256]{1,0:T(8,128)S(1)}, u32[]{:S(2)}, u32[]{:S(2)}) %collective-permute-start) | collective-permute-done | bytes 1572896 | tf_op jit(solution)/shard_map/ppermute | solution.py:12
  197.1 1.7 fusion.2
  198.8 0.0 copy-start.2
  198.8 0.0 reduce-scatter.2.cloned.1.call-update
  198.8 0.0 all-reduce.2.cloned.1.call-start
  198.9 25.0 %reduce-scatter.2.cloned.1.call-done = f32[768,256]{1,0:T(8,128)} async-done(((f32[1536,256]{1,0:T(8,128)}), f32[768,256]{1,0:T(8,128)}) %reduce-scatter.2.cloned.1.call-update) | async-done | bytes 786448 | tf_op jit(solution)/shard_map/reduce_scatter | solution.py:29
  223.8 0.0 copy-done.2
  223.8 0.0 copy-start.1
  223.8 2.2 fusion.4
  226.0 0.0 all-reduce.2.cloned.1.call-update
  226.1 0.0 copy-done
  226.1 0.0 copy-done.1
  226.1 1.1 fusion.3
  227.1 129.4 %all-reduce.2.cloned.1.call-done = f32[256,256]{1,0:T(8,128)} async-done(((f32[256,256]{1,0:T(8,128)}), f32[256,256]{1,0:T(8,128)}) %all-reduce.2.cloned.1.call-update) | async-done | bytes 262160 | tf_op jit(solution)/shard_map/psum | solution.py:34
  356.5 1.7 broadcast_multiply_fusion
  (1 shorter events, 0.0 us)
Async XLA Ops:
  7.2 218.9 %copy-start = (bf16[256,256]{1,0:T(8,128)(2,1)S(1)}, bf16[256,256]{1,0:T(8,128)(2,1)}, u32[]{:S(2)}) copy-start(bf16[256,256]{1,0:T(8,128)(2,1)} %param.10) | copy-start | bytes 393220
  7.2 216.7 %reduce-scatter.2.cloned.1.call-start = ((), (), s32[]{:S(2)}) async-start(), calls=%async_computation.1 | async-start | bytes 2359296 | tf_op jit(solution)/shard_map/reduce_scatter | solution.py:29
  43.5 4.1 %copy-start.3 = (s32[120]{0:T(128)S(1)}, s32[120]{0:T(128)}, u32[]{:S(2)}) copy-start(s32[120]{0:T(128)} %param.13) | copy-start | bytes 1444
  89.4 88.4 %collective-permute-start.3 = (f32[1536,256]{1,0:T(8,128)S(1)}, f32[1536,256]{1,0:T(8,128)S(1)}, u32[]{:S(2)}, u32[]{:S(2)}) collective-permute-start(f32[1536,256]{1,0:T(8,128)S(1)} %bitcast.22), channel_id=1, source_target_pairs={{0,4},{2,6},{4,8},{6,10},{8,12},{10,14},{12,16},{14,18},{16,20},{1... | collective-permute-start | bytes 4718600 | tf_op jit(solution)/shard_map/ppermute | solution.py:12
  92.5 85.3 %collective-permute-start.2 = (f32[1536,256]{1,0:T(8,128)S(1)}, f32[1536,256]{1,0:T(8,128)S(1)}, u32[]{:S(2)}, u32[]{:S(2)}) collective-permute-start(f32[1536,256]{1,0:T(8,128)S(1)} %bitcast.21), channel_id=1, source_target_pairs={{0,2},{2,4},{4,6},{6,8},{8,10},{10,12},{12,14},{14,16},{16,18},{18... | collective-permute-start | bytes 4718600 | tf_op jit(solution)/shard_map/ppermute | solution.py:12
  92.5 85.3 %collective-permute-start.1 = (f32[1536,256]{1,0:T(8,128)S(1)}, f32[1536,256]{1,0:T(8,128)S(1)}, u32[]{:S(2)}, u32[]{:S(2)}) collective-permute-start(f32[1536,256]{1,0:T(8,128)S(1)} %bitcast.20), channel_id=1, source_target_pairs={{0,30},{2,0},{4,2},{6,4},{8,6},{10,8},{12,10},{14,12},{16,14},{18,... | collective-permute-start | bytes 4718600 | tf_op jit(solution)/shard_map/ppermute | solution.py:12
  96.9 100.2 %collective-permute-start = (f32[1536,256]{1,0:T(8,128)S(1)}, f32[1536,256]{1,0:T(8,128)S(1)}, u32[]{:S(2)}, u32[]{:S(2)}) collective-permute-start(f32[1536,256]{1,0:T(8,128)S(1)} %bitcast.19), channel_id=1, source_target_pairs={{0,28},{2,30},{4,0},{6,2},{8,4},{10,6},{12,8},{14,10},{16,12},{18,... | collective-permute-start | bytes 4718600 | tf_op jit(solution)/shard_map/ppermute | solution.py:12
  198.8 25.0 %copy-start.2 = (bf16[768,256]{1,0:T(8,128)(2,1)S(1)}, bf16[768,256]{1,0:T(8,128)(2,1)}, u32[]{:S(2)}) copy-start(bf16[768,256]{1,0:T(8,128)(2,1)} %param.9) | copy-start | bytes 1179652
  198.8 157.7 %all-reduce.2.cloned.1.call-start = ((), (), s32[]{:S(2)}) async-start(), calls=%async_computation.2 | async-start | bytes 524288 | tf_op jit(solution)/shard_map/psum | solution.py:34
  223.8 2.3 copy-start.1
Sparse Core Ops, SparseCore 0:
  198.9 24.8 reduce-scatter.1
  229.9 126.5 all-reduce.1
where the time goes:
time: 365 us
  waiting for transfers between devices  254 us (70%)
  other arithmetic  43.5 us (12%)
  local copies, waits for them, and re-layouts  29.9 us (8%)
  matrix products  15.4 us (4%)
  between operations  14.1 us (4%)
  starting transfers between devices  7.82 us (2%)
    psum x1, waiting for transfers between devices, local(): lax.psum(weight_term, ('blk', 'rep')) * (1.0 / math.sqrt(node_count))  129 us
    ppermute x4, waiting for transfers between devices, shifted(): lax.ppermute(value, axis, [(i, (i + by) % devices) for i in range(devices)])  99.9 us
    scatter-add x1, other arithmetic, local(): jax.ops.segment_sum(tiles, block_cols, num_segments=spans * stripe_blocks)  38 us
    reduce_scatter x1, waiting for transfers between devices, local(): mine = lax.psum_scatter(total, 'rep', scatter_dimension=0, tiled=True)  25 us
    dot_general x1, local copies, waits for them, and re-layouts, local(): jnp.einsum('kab,kaf->kbf', block_values, picked, preferred_element_type=j...  15.6 us
    dot_general x1, matrix products, local(): jnp.einsum('kab,kaf->kbf', block_values, picked, preferred_element_type=j...  12.1 us
    ppermute x4, starting transfers between devices, shifted(): lax.ppermute(value, axis, [(i, (i + by) % devices) for i in range(devices)])  7.74 us
  transfers between devices with their start and end apart: 6, of which 4 were waited for; matrix products, arithmetic and copies ran while one was open for 0% of the time, Pallas kernels for 0%

commit v1 on v0

--- a/solution.py
+++ b/solution.py
@@ -31,7 +31,9 @@
     feats = jnp.maximum(prev_pre, jnp.zeros_like(prev_pre))
     weight_term = jnp.dot(feats.T, dy_rows, preferred_element_type=jnp.float32)
     node_count = stripe_rows * lax.axis_size("blk")
-    grad_weight = lax.psum(weight_term, ("blk", "rep")) * (1.0 / math.sqrt(node_count))
+    grad_weight = jnp.sum(lax.all_gather(weight_term, ("blk", "rep")), axis=0) * (
+        1.0 / math.sqrt(node_count)
+    )
     grad_in = (
         jnp.dot(dy_rows, weight.T, preferred_element_type=jnp.float32)
         * (prev_pre > 0).astype(jnp.float32)

time: 365 us -> 316 us (0.87)
  waiting for transfers between devices: 254 us -> 202 us
    psum x1 -> x0, waiting for transfers between devices: 129 us -> none  [local(): lax.psum(weight_term, ('blk', 'rep')) * (1.0 / math.sqrt(node_count))]
    all_gather x0 -> x1, waiting for transfers between devices: none -> 77.4 us  [local(): lax.all_gather(weight_term, ('blk', 'rep'))]
    reduce_sum x0 -> x1, other arithmetic: none -> 3.93 us  [local(): jnp.sum(lax.all_gather(weight_term, ('blk', 'rep')), axis=0)]
where the time goes in v1:
time: 316 us
  waiting for transfers between devices  202 us (64%)
  other arithmetic  46.5 us (15%)
  local copies, waits for them, and re-layouts  29.9 us (9%)
  matrix products  15.4 us (5%)
  between operations  14.1 us (4%)
  starting transfers between devices  7.82 us (2%)
    ppermute x4, waiting for transfers between devices, shifted(): lax.ppermute(value, axis, [(i, (i + by) % devices) for i in range(devices)])  99.9 us
    all_gather x1, waiting for transfers between devices, local(): lax.all_gather(weight_term, ('blk', 'rep'))  77.4 us
    scatter-add x1, other arithmetic, local(): jax.ops.segment_sum(tiles, block_cols, num_segments=spans * stripe_blocks)  38 us
    reduce_scatter x1, waiting for transfers between devices, local(): mine = lax.psum_scatter(total, 'rep', scatter_dimension=0, tiled=True)  25 us
    dot_general x1, local copies, waits for them, and re-layouts, local(): jnp.einsum('kab,kaf->kbf', block_values, picked, preferred_element_type=j...  15.6 us
    dot_general x1, matrix products, local(): jnp.einsum('kab,kaf->kbf', block_values, picked, preferred_element_type=j...  12.1 us
    ppermute x4, starting transfers between devices, shifted(): lax.ppermute(value, axis, [(i, (i + by) % devices) for i in range(devices)])  7.74 us
    gather x1, local copies, waits for them, and re-layouts, local(): picked = masked.reshape(stripe_blocks, block_size, width)[block_rows]  6.39 us
  transfers between devices with their start and end apart: 6, of which 4 were waited for; matrix products, arithmetic and copies ran while one was open for 0% of the time, Pallas kernels for 0%

profile of v1, /device:TPU:0, one launch (start us, length us, event | category | flops | bytes accessed | tf_op | source)
XLA Modules:
  0.0 316.0 jit_solution(16442731689333005880)
XLA Ops:
  7.2 0.0 copy-start
  7.2 0.0 reduce-scatter.2.cloned.1.call-start
  7.2 0.7 compare_select_fusion.1
  7.9 1.5 compare_select_fusion
  9.4 6.4 %gather_fusion = bf16[120,128,256]{2,1,0:T(8,128)(2,1)} fusion(bf16[12,128,256]{2,1,0:T(8,128)(2,1)S(1)} %bitcast.19, s32[1024]{0:T(1024)S(1)} %pad_clamp_fusion), kind=kCustom, calls=%fused_computation | custom fusion | bytes 15729120 | tf_op jit(solution)/shard_map/gather | solution.py:21
  15.8 12.1 %convolution_bitcast_fusion = f32[120,128,256]{1,2,0:T(8,128)} fusion(bf16[120,128,256]{2,1,0:T(8,128)(2,1)} %gather_fusion, bf16[120,128,128]{2,1,0:T(8,128)(2,1)} %param.11), kind=kOutput, calls=%fused_computation.2 | convolution fusion | flops 1006632960 | bytes 27525120 | tf_op jit(solution)/shard_map/kab,kaf->kbf/dot_general | solution.py:22
  27.9 15.6 %copy.11 = f32[120,128,256]{2,1,0:T(8,128)} copy(f32[120,128,256]{1,2,0:T(8,128)} %convolution_bitcast_fusion) | data formatting | bytes 31457280 | tf_op jit(solution)/shard_map/kab,kaf->kbf/dot_general | solution.py:22
  43.5 0.0 copy-start.3
  43.5 4.1 %broadcast_in_dim.9 = f32[60,128,256]{2,1,0:T(8,128)} broadcast(f32[]{:T(128)} %constant.6.clone.1), dimensions={} | broadcast | bytes 7864324 | tf_op jit(solution)/shard_map/broadcast_in_dim | solution.py:23
  47.5 0.0 copy-done.3
  47.5 38.0 %scatter_fusion = f32[60,128,256]{2,1,0:T(8,128)} fusion(f32[60,128,256]{2,1,0:T(8,128)} %broadcast_in_dim.9, s32[120]{0:T(128)S(1)} %copy-done.3, f32[120,128,256]{2,1,0:T(8,128)} %copy.11), kind=kCustom, calls=%fused_computation.1 | custom fusion | flops 3932160 | bytes 47186400 | tf_op jit(solution)/shard_map/scatter-add | solution.py:23
  85.6 3.9 %fusion.10 = (f32[12,128,256]{2,1,0:T(8,128)S(1)}, f32[12,128,256]{2,1,0:T(8,128)S(1)}, f32[12,128,256]{2,1,0:T(8,128)S(1)}, f32[12,128,256]{2,1,0:T(8,128)S(1)}, f32[12,128,256]{2,1,0:T(8,128)S(1)}) fusion(f32[60,128,256]{2,1,0:T(8,128)} %scatter_fusion), kind=kLoop, calls=%fused_computation.19 | loop fusion | bytes 15728640 | tf_op jit(solution)/shard_map/slice | solution.py:25
  89.4 3.0 collective-permute-start.3
  92.5 0.0 collective-permute-start.2
  92.5 4.4 %collective-permute-start.1 = (f32[1536,256]{1,0:T(8,128)S(1)}, f32[1536,256]{1,0:T(8,128)S(1)}, u32[]{:S(2)}, u32[]{:S(2)}) collective-permute-start(f32[1536,256]{1,0:T(8,128)S(1)} %bitcast.22), channel_id=1, source_target_pairs={{0,30},{2,0},{4,2},{6,4},{8,6},{10,8},{12,10},{14,12},{16,14},{18,... | collective-permute-start | bytes 4718600 | tf_op jit(solution)/shard_map/ppermute | solution.py:12
  96.9 0.3 collective-permute-start
  97.2 80.6 %collective-permute-done.3 = f32[1536,256]{1,0:T(8,128)S(1)} collective-permute-done((f32[1536,256]{1,0:T(8,128)S(1)}, f32[1536,256]{1,0:T(8,128)S(1)}, u32[]{:S(2)}, u32[]{:S(2)}) %collective-permute-start.3) | collective-permute-done | bytes 1572896 | tf_op jit(solution)/shard_map/ppermute | solution.py:12
  177.8 0.0 collective-permute-done.2
  177.8 0.0 collective-permute-done.1
  177.8 19.3 %collective-permute-done = f32[1536,256]{1,0:T(8,128)S(1)} collective-permute-done((f32[1536,256]{1,0:T(8,128)S(1)}, f32[1536,256]{1,0:T(8,128)S(1)}, u32[]{:S(2)}, u32[]{:S(2)}) %collective-permute-start) | collective-permute-done | bytes 1572896 | tf_op jit(solution)/shard_map/ppermute | solution.py:12
  197.1 1.7 fusion.2
  198.8 0.0 copy-start.2
  198.8 0.0 reduce-scatter.2.cloned.1.call-update
  198.8 0.0 all-gather.3.cloned.1.call-start
  198.9 25.0 %reduce-scatter.2.cloned.1.call-done = f32[768,256]{1,0:T(8,128)} async-done(((f32[1536,256]{1,0:T(8,128)}), f32[768,256]{1,0:T(8,128)}) %reduce-scatter.2.cloned.1.call-update) | async-done | bytes 786448 | tf_op jit(solution)/shard_map/reduce_scatter | solution.py:29
  223.8 0.0 copy-done.2
  223.8 0.0 copy-start.1
  223.8 2.2 fusion.4
  226.0 0.0 all-gather.3.cloned.1.call-update
  226.1 0.0 copy-done
  226.1 0.0 copy-done.1
  226.1 1.1 fusion.3
  227.1 77.4 %all-gather.3.cloned.1.call-done = f32[8192,256]{1,0:T(8,128)} async-done(((f32[256,256]{1,0:T(8,128)}), f32[8192,256]{1,0:T(8,128)}) %all-gather.3.cloned.1.call-update) | async-done | bytes 8388624 | tf_op jit(solution)/shard_map/all_gather | solution.py:34
  304.5 3.9 %reduce_sum.9 = f32[256,256]{1,0:T(8,128)S(1)} reduce(f32[32,256,256]{2,1,0:T(8,128)} %bitcast.20, f32[]{:T(128)} %constant.6.clone.1), dimensions={0}, to_apply=%region_2.0 | reduce | flops 2031616 | bytes 8650756 | tf_op jit(solution)/shard_map/reduce_sum | solution.py:34
  308.4 0.7 broadcast_multiply_fusion
  (1 shorter events, 0.0 us)
Async XLA Ops:
  7.2 218.9 %copy-start = (bf16[256,256]{1,0:T(8,128)(2,1)S(1)}, bf16[256,256]{1,0:T(8,128)(2,1)}, u32[]{:S(2)}) copy-start(bf16[256,256]{1,0:T(8,128)(2,1)} %param.10) | copy-start | bytes 393220
  7.2 216.7 %reduce-scatter.2.cloned.1.call-start = ((), (), s32[]{:S(2)}) async-start(), calls=%async_computation.1 | async-start | bytes 2359296 | tf_op jit(solution)/shard_map/reduce_scatter | solution.py:29
  43.5 4.1 %copy-start.3 = (s32[120]{0:T(128)S(1)}, s32[120]{0:T(128)}, u32[]{:S(2)}) copy-start(s32[120]{0:T(128)} %param.13) | copy-start | bytes 1444
  89.4 88.4 %collective-permute-start.3 = (f32[1536,256]{1,0:T(8,128)S(1)}, f32[1536,256]{1,0:T(8,128)S(1)}, u32[]{:S(2)}, u32[]{:S(2)}) collective-permute-start(f32[1536,256]{1,0:T(8,128)S(1)} %bitcast.24), channel_id=1, source_target_pairs={{0,4},{2,6},{4,8},{6,10},{8,12},{10,14},{12,16},{14,18},{16,20},{1... | collective-permute-start | bytes 4718600 | tf_op jit(solution)/shard_map/ppermute | solution.py:12
  92.5 85.3 %collective-permute-start.2 = (f32[1536,256]{1,0:T(8,128)S(1)}, f32[1536,256]{1,0:T(8,128)S(1)}, u32[]{:S(2)}, u32[]{:S(2)}) collective-permute-start(f32[1536,256]{1,0:T(8,128)S(1)} %bitcast.23), channel_id=1, source_target_pairs={{0,2},{2,4},{4,6},{6,8},{8,10},{10,12},{12,14},{14,16},{16,18},{18... | collective-permute-start | bytes 4718600 | tf_op jit(solution)/shard_map/ppermute | solution.py:12
  92.5 85.3 %collective-permute-start.1 = (f32[1536,256]{1,0:T(8,128)S(1)}, f32[1536,256]{1,0:T(8,128)S(1)}, u32[]{:S(2)}, u32[]{:S(2)}) collective-permute-start(f32[1536,256]{1,0:T(8,128)S(1)} %bitcast.22), channel_id=1, source_target_pairs={{0,30},{2,0},{4,2},{6,4},{8,6},{10,8},{12,10},{14,12},{16,14},{18,... | collective-permute-start | bytes 4718600 | tf_op jit(solution)/shard_map/ppermute | solution.py:12
  96.9 100.2 %collective-permute-start = (f32[1536,256]{1,0:T(8,128)S(1)}, f32[1536,256]{1,0:T(8,128)S(1)}, u32[]{:S(2)}, u32[]{:S(2)}) collective-permute-start(f32[1536,256]{1,0:T(8,128)S(1)} %bitcast.21), channel_id=1, source_target_pairs={{0,28},{2,30},{4,0},{6,2},{8,4},{10,6},{12,8},{14,10},{16,12},{18,... | collective-permute-start | bytes 4718600 | tf_op jit(solution)/shard_map/ppermute | solution.py:12
  198.8 25.0 %copy-start.2 = (bf16[768,256]{1,0:T(8,128)(2,1)S(1)}, bf16[768,256]{1,0:T(8,128)(2,1)}, u32[]{:S(2)}) copy-start(bf16[768,256]{1,0:T(8,128)(2,1)} %param.9) | copy-start | bytes 1179652
  198.8 105.7 %all-gather.3.cloned.1.call-start = ((), (), s32[]{:S(2)}) async-start(), calls=%async_computation.2 | async-start | bytes 8650752 | tf_op jit(solution)/shard_map/all_gather | solution.py:34
  223.8 2.3 copy-start.1
Sparse Core Ops, SparseCore 0:
  198.9 24.8 reduce-scatter.1
  227.4 77.0 all-gather.2
